TPU v7x, 32 devices: a whole 2x2x4 slice. The times are simulated.
32 devices in a mesh: seq: 2 (over z_hi), fsdp: 8 (over y, x, core), dp: 2 (over z_lo).
Axes of the slice: x: 2, y: 2, z: 4 (z_hi: 2, z_lo: 2; z = z_hi * 2 + z_lo), core: 2. Of those that a mesh axis runs over, the one named last changes fastest.
Arguments:
- images: bfloat16 [48, 584, 1024], P(('fsdp', 'dp'), 'seq'), may hold values from -6 to 6
- key_mask: int32 [48, 584], P(('fsdp', 'dp')), may hold values from 0 to 1, as said below
- out_grad: bfloat16 [48, 584, 1024], P(('fsdp', 'dp'), 'seq'), may hold values from -6 to 6
- step_count: int32 [], replicated, may hold values from 2 to 20
- in_weights: float32 [1024, 3072], P(('seq', 'fsdp')), may hold values from -0.25 to 0.25
- out_weights: float32 [1024, 1024], P(('seq', 'fsdp')), may hold values from -0.375 to 0.375
- up_weights: float32 [4096, 1024], P(('seq', 'fsdp')), may hold values from -0.1875 to 0.1875
- down_weights: float32 [4096, 1024], P(('seq', 'fsdp')), may hold values from -0.09375 to 0.09375
- vectors: float32 [12288], P(('seq', 'fsdp')), may hold values from -0.4 to 1.4
- first_in: float32 [1024, 3072], P(('seq', 'fsdp')), may hold values from -1.5 to 1.5
- first_out: float32 [1024, 1024], P(('seq', 'fsdp')), may hold values from -0.9 to 0.9
- first_up: float32 [4096, 1024], P(('seq', 'fsdp')), may hold values from -2.2 to 2.2
- first_down: float32 [4096, 1024], P(('seq', 'fsdp')), may hold values from -4.5 to 4.5
- first_vectors: float32 [12288], P(('seq', 'fsdp')), may hold values from -4.5 to 4.5
- second_in: float32 [1024, 3072], P(('seq', 'fsdp')), may hold values from 0.03 to 0.25
- second_out: float32 [1024, 1024], P(('seq', 'fsdp')), may hold values from 0.012 to 0.09
- second_up: float32 [4096, 1024], P(('seq', 'fsdp')), may hold values from 0.07 to 0.55
- second_down: float32 [4096, 1024], P(('seq', 'fsdp')), may hold values from 0.28 to 2.2
- second_vectors: float32 [12288], P(('seq', 'fsdp')), may hold values from 0.28 to 2.2
Outputs:
- grad_norm: float32 [], replicated
- new_in: float32 [1024, 3072], P(('seq', 'fsdp'))
- new_out: float32 [1024, 1024], P(('seq', 'fsdp'))
- new_up: float32 [4096, 1024], P(('seq', 'fsdp'))
- new_down: float32 [4096, 1024], P(('seq', 'fsdp'))
- new_vectors: float32 [12288], P(('seq', 'fsdp'))
- first_in_new: float32 [1024, 3072], P(('seq', 'fsdp'))
- first_out_new: float32 [1024, 1024], P(('seq', 'fsdp'))
- first_up_new: float32 [4096, 1024], P(('seq', 'fsdp'))
- first_down_new: float32 [4096, 1024], P(('seq', 'fsdp'))
- first_vectors_new: float32 [12288], P(('seq', 'fsdp'))
- second_in_new: float32 [1024, 3072], P(('seq', 'fsdp'))
- second_out_new: float32 [1024, 1024], P(('seq', 'fsdp'))
- second_up_new: float32 [4096, 1024], P(('seq', 'fsdp'))
- second_down_new: float32 [4096, 1024], P(('seq', 'fsdp'))
- second_vectors_new: float32 [12288], P(('seq', 'fsdp'))
- copy_in: bfloat16 [1024, 3072], P(('seq', 'fsdp'))
- copy_out: bfloat16 [1024, 1024], P(('seq', 'fsdp'))
- copy_up: bfloat16 [4096, 1024], P(('seq', 'fsdp'))
- copy_down: bfloat16 [4096, 1024], P(('seq', 'fsdp'))
- copy_vectors: bfloat16 [12288], P(('seq', 'fsdp'))
- activations: float32 [48, 584, 1024], P(('fsdp', 'dp'), 'seq')
- input_grad: float32 [48, 584, 1024], P(('fsdp', 'dp'), 'seq')
Inputs may be any that keep to these rules, and one draw needn't show every extreme that they name: `key_mask`: every image has exactly 577 ones; where its 7 zeros stand is drawn afresh for each image.
All inputs are finite; a program needn't handle non-finite values.
Results may differ from a plain program's by a relative error of at most 0.02.
The roundings to bfloat16 on the way count: a program that leaves them out, or rounds other values in their place, can miss the bound.
Values may be sent and summed in bfloat16 or wider, within the bound.
A program may use at most 256 MiB of HBM per device.

v0:
```python
import math
import jax
import jax.numpy as jnp
from jax import lax
from jax.sharding import PartitionSpec as P

D = 1024
HD = 64
FF = 4096
NEG_FILL = -1000000000.0
NORM_EPS = 1e-06
ADAM_EPS = 1e-08
WEIGHT_DECAY = 0.05


def layer_norm(values, norm_gain, norm_shift):
    center = values - jnp.mean(values, axis=-1, keepdims=True)
    spread = jnp.mean(center * center, axis=-1, keepdims=True)
    return center * lax.rsqrt(spread + NORM_EPS) * norm_gain + norm_shift


def gelu_tanh(values):
    return jax.nn.gelu(values, approximate=True)


def matmul(former, latter):
    return jnp.dot(former, latter, preferred_element_type=jnp.float32)


def by_rows(former, latter):
    return lax.dot_general(
        former, latter, (((0,), (0,)), ((), ())), preferred_element_type=jnp.float32
    )


def by_columns(former, latter):
    return lax.dot_general(
        former, latter, (((1,), (1,)), ((), ())), preferred_element_type=jnp.float32
    )


def split_heads(head_block):
    token_count = head_block.shape[0]
    local_heads = head_block.shape[2] // HD
    queries = head_block[:, 0].reshape(token_count, local_heads, HD)
    key_rows = head_block[:, 1].reshape(token_count, local_heads, HD)
    value_rows = head_block[:, 2].reshape(token_count, local_heads, HD)
    return (queries, key_rows, value_rows)


def masked_scores(queries, key_rows, mask_row):
    scores = jnp.einsum(
        "qhd,khd->hqk", queries, key_rows, preferred_element_type=jnp.float32
    ) * HD ** (-0.5)
    return jnp.where((mask_row > 0)[None, None, :], scores, NEG_FILL)


def attend_image(packed_item):
    head_block, mask_row = packed_item
    queries, key_rows, value_rows = split_heads(head_block)
    scores = masked_scores(queries, key_rows, mask_row)
    row_max = jnp.max(scores, axis=-1, keepdims=True)
    exponent = jnp.exp(scores - row_max)
    row_total = jnp.sum(exponent, axis=-1, keepdims=True)
    attention = (exponent / row_total).astype(jnp.bfloat16)
    log_totals = (row_max + jnp.log(row_total))[..., 0]
    mixed = jnp.einsum("hqk,khd->qhd", attention, value_rows, preferred_element_type=jnp.float32)
    token_count = head_block.shape[0]
    return (mixed.reshape(token_count, head_block.shape[2]).astype(jnp.bfloat16), log_totals)


def attend_back(packed_item):
    head_block, log_totals, mask_row, grad_mixed = packed_item
    queries, key_rows, value_rows = split_heads(head_block)
    token_count = head_block.shape[0]
    local_heads = head_block.shape[2] // HD
    scores = masked_scores(queries, key_rows, mask_row)
    attention = jnp.exp(scores - log_totals[..., None])
    grad_view = grad_mixed.reshape(token_count, local_heads, HD)
    grad_attention = jnp.einsum(
        "qhd,khd->hqk", grad_view, value_rows, preferred_element_type=jnp.float32
    )
    row_delta = jnp.sum(attention * grad_attention, axis=-1, keepdims=True)
    grad_scores = jnp.where(
        (mask_row > 0)[None, None, :], attention * (grad_attention - row_delta), 0.0
    ).astype(jnp.bfloat16)
    grad_queries = jnp.einsum(
        "hqk,khd->qhd", grad_scores, key_rows, preferred_element_type=jnp.float32
    ) * HD ** (-0.5)
    grad_keys = jnp.einsum(
        "hqk,qhd->khd", grad_scores, queries, preferred_element_type=jnp.float32
    ) * HD ** (-0.5)
    grad_values = jnp.einsum(
        "hqk,qhd->khd",
        attention.astype(jnp.bfloat16),
        grad_view,
        preferred_element_type=jnp.float32,
    )
    stacked = jnp.stack([grad_queries, grad_keys, grad_values], axis=1)
    return stacked.reshape(token_count, 3, head_block.shape[2]).astype(jnp.bfloat16)


def adam_update(master, first_moment, second_moment, gradient, step_rate, bias_one, bias_two):
    first_new = 0.5 * first_moment + 0.5 * gradient
    second_new = 0.5 * second_moment + 0.5 * gradient * gradient
    update = first_new / bias_one / (jnp.sqrt(second_new / bias_two) + ADAM_EPS)
    master_new = master - step_rate * (update + WEIGHT_DECAY * master)
    return (master_new, first_new, second_new)


def on_device(
    images,
    key_mask,
    out_grad,
    step_count,
    in_weights,
    out_weights,
    up_weights,
    down_weights,
    vectors,
    first_in,
    first_out,
    first_up,
    first_down,
    first_vectors,
    second_in,
    second_out,
    second_up,
    second_down,
    second_vectors,
):
    full_in, full_out, full_vec = (
        lax.all_gather(in_weights.astype(jnp.bfloat16), ("seq", "fsdp"), axis=0, tiled=True),
        lax.all_gather(out_weights.astype(jnp.bfloat16), ("seq", "fsdp"), axis=0, tiled=True),
        lax.all_gather(vectors.astype(jnp.bfloat16), ("seq", "fsdp"), axis=0, tiled=True),
    )
    full_up, full_down = (
        lax.all_gather(up_weights.astype(jnp.bfloat16), ("seq", "fsdp"), axis=0, tiled=True),
        lax.all_gather(down_weights.astype(jnp.bfloat16), ("seq", "fsdp"), axis=0, tiled=True),
    )
    image_count, half_tokens, features = images.shape
    row_count = image_count * half_tokens
    vector_copy = full_vec.astype(jnp.float32)
    gain_one = vector_copy[0:features]
    shift_one = vector_copy[features : 2 * features]
    query_bias = vector_copy[2 * features : 3 * features]
    value_bias = vector_copy[3 * features : 4 * features]
    out_bias = vector_copy[4 * features : 5 * features]
    gain_two = vector_copy[5 * features : 6 * features]
    shift_two = vector_copy[6 * features : 7 * features]
    down_bias = vector_copy[7 * features : 8 * features]
    up_bias = vector_copy[8 * features :]
    in_bias = jnp.concatenate([query_bias, jnp.zeros_like(query_bias), value_bias])
    flat_input = images.reshape(row_count, features).astype(jnp.float32)
    normed_one = layer_norm(flat_input, gain_one, shift_one).astype(jnp.bfloat16)
    packed = (matmul(normed_one, full_in) + in_bias).astype(jnp.bfloat16)
    packed = packed.reshape(image_count, half_tokens, 3, features)
    head_packed = lax.all_to_all(packed, "seq", split_axis=3, concat_axis=1, tiled=True)
    mixed_heads, log_totals = lax.map(attend_image, (head_packed, key_mask))
    mixed = lax.all_to_all(mixed_heads, "seq", split_axis=1, concat_axis=2, tiled=True).reshape(
        row_count, features
    )
    middle = flat_input + matmul(mixed, full_out) + out_bias
    normed_two = layer_norm(middle, gain_two, shift_two).astype(jnp.bfloat16)
    grad_result = out_grad.reshape(row_count, features)
    grad_result_wide = grad_result.astype(jnp.float32)
    grad_down_b = jnp.sum(grad_result_wide, axis=0)
    hidden_input = by_columns(normed_two, full_up) + up_bias
    hidden = gelu_tanh(hidden_input).astype(jnp.bfloat16)
    result = middle + matmul(hidden, full_down) + down_bias
    grad_down_w = by_rows(hidden, grad_result)
    grad_hidden = by_columns(grad_result, full_down)
    unused_value, gelu_back = jax.vjp(gelu_tanh, hidden_input)
    grad_hidden_in = gelu_back(grad_hidden)[0].astype(jnp.bfloat16)
    grad_up_b = jnp.sum(grad_hidden_in.astype(jnp.float32), axis=0)
    grad_up_w = by_rows(grad_hidden_in, normed_two)
    grad_normed_two = matmul(grad_hidden_in, full_up)
    unused_two, norm_back_two = jax.vjp(layer_norm, middle, gain_two, shift_two)
    grad_middle_norm, grad_gain_two, grad_shift_two = norm_back_two(grad_normed_two)
    grad_middle = grad_result_wide + grad_middle_norm
    grad_branch = grad_middle.astype(jnp.bfloat16)
    grad_out_b = jnp.sum(grad_branch.astype(jnp.float32), axis=0)
    grad_out_w = by_rows(mixed, grad_branch)
    grad_mixed = (
        by_columns(grad_branch, full_out)
        .astype(jnp.bfloat16)
        .reshape(image_count, half_tokens, features)
    )
    grad_heads = lax.all_to_all(grad_mixed, "seq", split_axis=2, concat_axis=1, tiled=True)
    grad_packed_heads = lax.map(attend_back, (head_packed, log_totals, key_mask, grad_heads))
    grad_packed = lax.all_to_all(
        grad_packed_heads, "seq", split_axis=1, concat_axis=3, tiled=True
    ).reshape(row_count, 3 * features)
    grad_in_w = by_rows(normed_one, grad_packed)
    column_sums = jnp.sum(grad_packed.astype(jnp.float32), axis=0)
    grad_query_b = column_sums[0:features]
    grad_value_b = column_sums[2 * features :]
    grad_normed_one = by_columns(grad_packed, full_in)
    unused_one, norm_back_one = jax.vjp(layer_norm, flat_input, gain_one, shift_one)
    grad_input_norm, grad_gain_one, grad_shift_one = norm_back_one(grad_normed_one)
    input_grad = grad_middle + grad_input_norm
    grad_vec = jnp.concatenate(
        [
            grad_gain_one,
            grad_shift_one,
            grad_query_b,
            grad_value_b,
            grad_out_b,
            grad_gain_two,
            grad_shift_two,
            grad_down_b,
            grad_up_b,
        ]
    )
    share_in, share_out, share_vec = (
        lax.psum_scatter(grad_in_w, ("seq", "fsdp"), scatter_dimension=0, tiled=True),
        lax.psum_scatter(grad_out_w, ("seq", "fsdp"), scatter_dimension=0, tiled=True),
        lax.psum_scatter(grad_vec, ("seq", "fsdp"), scatter_dimension=0, tiled=True),
    )
    share_up, share_down = (
        lax.psum_scatter(grad_up_w, ("seq", "fsdp"), scatter_dimension=0, tiled=True),
        lax.psum_scatter(grad_down_w, ("seq", "fsdp"), scatter_dimension=0, tiled=True),
    )
    share_in, share_out, share_up, share_down, share_vec = (
        lax.psum(share_in.astype(jnp.bfloat16), "dp").astype(jnp.float32),
        lax.psum(share_out.astype(jnp.bfloat16), "dp").astype(jnp.float32),
        lax.psum(share_up.astype(jnp.bfloat16), "dp").astype(jnp.float32),
        lax.psum(share_down.astype(jnp.bfloat16), "dp").astype(jnp.float32),
        lax.psum(share_vec.astype(jnp.bfloat16), "dp").astype(jnp.float32),
    )
    shares = (share_in, share_out, share_up, share_down, share_vec)
    square_part = (
        jnp.sum(share_in * share_in)
        + jnp.sum(share_out * share_out)
        + jnp.sum(share_up * share_up)
        + jnp.sum(share_down * share_down)
        + jnp.sum(share_vec * share_vec)
    )
    square_total = lax.psum(square_part, ("seq", "fsdp"))
    grad_norm = jnp.sqrt(square_total)
    threshold = 0.5 * math.sqrt(4 * D * D + 2 * D * FF + 12 * D)
    clip_factor = jnp.minimum(1.0, threshold / grad_norm)
    decay_power = jnp.power(jnp.float32(0.5), step_count.astype(jnp.float32))
    bias_one = 1.0 - decay_power
    bias_two = 1.0 - decay_power
    rates = ((D // 2) ** (-0.5), (D // 4) ** (-0.5), D ** (-0.5), FF ** (-0.5), 0.2)
    masters = (in_weights, out_weights, up_weights, down_weights, vectors)
    firsts = (first_in, first_out, first_up, first_down, first_vectors)
    seconds = (second_in, second_out, second_up, second_down, second_vectors)
    results = [
        adam_update(
            masters[index],
            firsts[index],
            seconds[index],
            shares[index] * clip_factor,
            rates[index],
            bias_one,
            bias_two,
        )
        for index in range(5)
    ]
    new_masters = [entry[0] for entry in results]
    new_firsts = [entry[1] for entry in results]
    new_seconds = [entry[2] for entry in results]
    copies = [master.astype(jnp.bfloat16) for master in new_masters]
    activations = result.reshape(image_count, half_tokens, features)
    input_grad = input_grad.reshape(image_count, half_tokens, features)
    return (
        grad_norm,
        new_masters[0],
        new_masters[1],
        new_masters[2],
        new_masters[3],
        new_masters[4],
        new_firsts[0],
        new_firsts[1],
        new_firsts[2],
        new_firsts[3],
        new_firsts[4],
        new_seconds[0],
        new_seconds[1],
        new_seconds[2],
        new_seconds[3],
        new_seconds[4],
        copies[0],
        copies[1],
        copies[2],
        copies[3],
        copies[4],
        activations,
        input_grad,
    )


def solution(mesh):
    placed = (
        P(("fsdp", "dp"), "seq", None),
        P(("fsdp", "dp"), None),
        P(("fsdp", "dp"), "seq", None),
        P(),
        P(("seq", "fsdp"), None),
        P(("seq", "fsdp"), None),
        P(("seq", "fsdp"), None),
        P(("seq", "fsdp"), None),
        P(("seq", "fsdp")),
        P(("seq", "fsdp"), None),
        P(("seq", "fsdp"), None),
        P(("seq", "fsdp"), None),
        P(("seq", "fsdp"), None),
        P(("seq", "fsdp")),
        P(("seq", "fsdp"), None),
        P(("seq", "fsdp"), None),
        P(("seq", "fsdp"), None),
        P(("seq", "fsdp"), None),
        P(("seq", "fsdp")),
    )
    return jax.shard_map(
        on_device,
        mesh=mesh,
        in_specs=placed,
        out_specs=(
            P(),
            P(("seq", "fsdp"), None),
            P(("seq", "fsdp"), None),
            P(("seq", "fsdp"), None),
            P(("seq", "fsdp"), None),
            P(("seq", "fsdp")),
            P(("seq", "fsdp"), None),
            P(("seq", "fsdp"), None),
            P(("seq", "fsdp"), None),
            P(("seq", "fsdp"), None),
            P(("seq", "fsdp")),
            P(("seq", "fsdp"), None),
            P(("seq", "fsdp"), None),
            P(("seq", "fsdp"), None),
            P(("seq", "fsdp"), None),
            P(("seq", "fsdp")),
            P(("seq", "fsdp"), None),
            P(("seq", "fsdp"), None),
            P(("seq", "fsdp"), None),
            P(("seq", "fsdp"), None),
            P(("seq", "fsdp")),
            P(("fsdp", "dp"), "seq", None),
            P(("fsdp", "dp"), "seq", None),
        ),
        check_vma=False,
    )
```

profile of v0, /device:TPU:0, one launch (start us, length us, event | category | flops | bytes accessed | tf_op | source)
XLA Modules:
  0.0 1772.8 jit_solution(14183998428511871880)
XLA Ops:
  17.8 23.3 %all-gather = bf16[16,1,768]{2,1,0:T(2,128)(2,1)S(1)} all-gather(bf16[1,1,768]{2,1,0:T(2,128)(2,1)S(1)} %reshape.302), channel_id=1, replica_groups=mesh['seq'=2,'fsdp'=8,'dp'=2] {'seq','fsdp'}, dimensions={0}, use_global_device_ids=true | all-gather | bytes 26112 | tf_op jit(solution)/shard_map/all_gather | solution.py:135
  42.4 39.8 %all-gather.6.cloned.1.call-done = bf16[1024,3072]{1,0:T(8,128)(2,1)} async-done(((bf16[64,3072]{1,0:T(8,128)(2,1)}), bf16[1024,3072]{1,0:T(8,128)(2,1)}) %all-gather.6.cloned.1.call-update) | async-done | bytes 6291472 | tf_op jit(solution)/shard_map/all_gather | solution.py:133
  82.2 11.2 add_convert_fusion
  93.5 16.3 reshape.294
  109.8 18.0 %copy.98 = bf16[3,292,3,1024]{1,2,0,3:T(4,128)(2,1)} copy(bf16[3,292,3,1024]{3,2,1,0:T(4,128)(2,1)} %reshape.294) | data formatting | bytes 10764288 | tf_op jit(solution)/shard_map/reshape | solution.py:157
  127.8 7.5 all-to-all-start
  136.5 308.5 %all-to-all-done = bf16[3,292,3,1024]{1,2,0,3:T(4,128)(2,1)} async-done(((bf16[3,292,3,1024]{1,2,0,3:T(4,128)(2,1)}), bf16[3,292,3,1024]{1,2,0,3:T(4,128)(2,1)}, u32[]{:S(2)}, u32[]{:S(2)}) %all-to-all-start) | async-done | bytes 5382176 | tf_op jit(solution)/shard_map/all_to_all | solution.py:158
  445.0 14.7 copy.135
  459.7 14.5 reshape.307
  474.2 32.3 %while.22 = (s32[]{:T(128)}, bf16[3,584,512]{1,2,0:T(8,128)(2,1)S(1)}, f32[3,8,584]{2,1,0:T(8,128)S(1)}, bf16[3,584,3,512]{1,3,2,0:T(8,128)(2,1)}, s32[3,584]{1,0:T(4,128)S(1)}, /*index=5*/s32[]{:T(128)}) while((s32[]{:T(128)}, bf16[3,584,512]{1,2,0:T(8,128)(2,1)S(1)}, f32[3,8,584]{2,1,0:T(8,128)S(1)}, bf16[3,584,3,512]{1,3,2,0:T(8,128)(2,1)}, ...), condition=%wide.region_5.6_spmd, body=%wide.region_2.5_spmd.sunk | while | flops 731518976 | bytes 43779996 | solution.py:159
  481.5 3.3 fusion.172
  486.9 2.8 fusion.170
  492.3 3.3 fusion.172
  497.7 2.8 fusion.170
  503.1 3.3 fusion.172
  506.5 3.7 copy.102
  510.2 5.4 all-to-all-start.1
  518.0 43.1 %all-to-all-done.1 = bf16[3,584,512]{2,0,1:T(4,128)(2,1)} async-done(((bf16[3,584,512]{2,0,1:T(4,128)(2,1)}), bf16[3,584,512]{2,0,1:T(4,128)(2,1)}, u32[]{:S(2)}, u32[]{:S(2)}) %all-to-all-start.1) | async-done | bytes 1794080 | tf_op jit(solution)/shard_map/all_to_all | solution.py:160
  567.7 5.3 fusion.109
  575.4 15.2 fusion.90
  590.5 22.0 %convert_reduce_fusion = (f32[4096]{0:T(1024)}, bf16[876,4096]{1,0:T(8,128)(2,1)}) fusion(f32[876,4096]{1,0:T(8,128)} %fusion.90, f32[4096]{0:T(1024)S(1)} %slice.83, bf16[876,1024]{1,0:T(8,128)(2,1)S(1)} %reshape.295, bf16[4096,1024]{1,0:T(8,128)(2,1)} %all-gather.8.cloned.1.call-done), kind=kOutput, calls=%fused_computation.60 | convolution fusion | flops 7430942720 | bytes 31744000 | tf_op jit(solution)/shard_map/dot_general | solution.py:37
  612.6 13.6 multiply_reduce_fusion.3
  631.7 3.3 convolution_convert_fusion
  636.6 3.9 copy.105
  640.5 3.9 all-to-all-start.2
  644.5 6.4 fusion.113
  651.0 89.5 %all-to-all-done.2 = bf16[3,292,1024]{1,0,2:T(4,128)(2,1)S(1)} async-done(((bf16[3,292,1024]{1,0,2:T(4,128)(2,1)}), bf16[3,292,1024]{1,0,2:T(4,128)(2,1)S(1)}, u32[]{:S(2)}, u32[]{:S(2)}) %all-to-all-start.2) | async-done | bytes 1794080 | tf_op jit(solution)/shard_map/all_to_all | solution.py:189
  740.5 4.2 copy.136
  744.7 5.8 reshape.305
  750.5 183.9 %while.23 = (s32[]{:T(128)}, bf16[3,584,3,512]{1,3,2,0:T(8,128)(2,1)}, bf16[3,584,3,512]{1,3,2,0:T(8,128)(2,1)}, s32[3,584]{1,0:T(4,128)S(1)}, f32[3,8,584]{2,1,...) while((s32[]{:T(128)}, bf16[3,584,3,512]{1,3,2,0:T(8,128)(2,1)}, ...), condition=%wide.region_12.13_spmd, body=%wide.region_10.12_spmd.sunk | while | flops 1824034688 | bytes 138262480 | solution.py:190
  756.1 2.8 fusion.185
  760.4 6.4 fusion.186
  766.8 21.8 %fusion.188 = bf16[8,64,584]{2,1,0:T(8,128)(2,1)S(1)} fusion(bf16[584,8,64]{0,2,1:T(8,128)(2,1)S(1)} %bitcast.145, f32[8,584,584]{1,2,0:T(8,128)} %fusion.186, f32[8,584,584]{1,2,0:T(8,128)} %copy-done, f32[8,584]{1,0:T(8,128)S(1)} %dynamic-slice_bitcast_fusion.8, pred[584]{0:T(1024)(128)(4,1)S(1)} %compare_reduce_fusion.5), kind=kOutput, calls=%fused_computation.38.clone.1 | convolution fusion | flops 379857536 | bytes 23042888 | tf_op jit(solution)/shard_map/while/body/eval_jaxpr/hqk,khd->qhd/dot_general | solution.py:87
  788.6 21.9 %fusion.187 = bf16[8,64,584]{2,1,0:T(8,128)(2,1)S(1)} fusion(bf16[584,8,64]{0,2,1:T(8,128)(2,1)S(1)} %bitcast.143, f32[8,584,584]{1,2,0:T(8,128)} %fusion.186, f32[8,584,584]{1,2,0:T(8,128)} %copy-done, f32[8,584]{1,0:T(8,128)S(1)} %dynamic-slice_bitcast_fusion.8, pred[584]{0:T(1024)(128)(4,1)S(1)} %compare_reduce_fusion.5), kind=kOutput, calls=%fused_computation.37.clone.1 | convolution fusion | flops 379857536 | bytes 23042888 | tf_op jit(solution)/shard_map/while/body/eval_jaxpr/hqk,qhd->khd/dot_general | solution.py:90
  817.2 2.8 fusion.185
  821.6 6.4 fusion.186
  827.9 21.8 %fusion.188 = bf16[8,64,584]{2,1,0:T(8,128)(2,1)S(1)} fusion(bf16[584,8,64]{0,2,1:T(8,128)(2,1)S(1)} %bitcast.145, f32[8,584,584]{1,2,0:T(8,128)} %fusion.186, f32[8,584,584]{1,2,0:T(8,128)} %copy-done, f32[8,584]{1,0:T(8,128)S(1)} %dynamic-slice_bitcast_fusion.8, pred[584]{0:T(1024)(128)(4,1)S(1)} %compare_reduce_fusion.5), kind=kOutput, calls=%fused_computation.38.clone.1 | convolution fusion | flops 379857536 | bytes 23042888 | tf_op jit(solution)/shard_map/while/body/eval_jaxpr/hqk,khd->qhd/dot_general | solution.py:87
  849.8 21.9 %fusion.187 = bf16[8,64,584]{2,1,0:T(8,128)(2,1)S(1)} fusion(bf16[584,8,64]{0,2,1:T(8,128)(2,1)S(1)} %bitcast.143, f32[8,584,584]{1,2,0:T(8,128)} %fusion.186, f32[8,584,584]{1,2,0:T(8,128)} %copy-done, f32[8,584]{1,0:T(8,128)S(1)} %dynamic-slice_bitcast_fusion.8, pred[584]{0:T(1024)(128)(4,1)S(1)} %compare_reduce_fusion.5), kind=kOutput, calls=%fused_computation.37.clone.1 | convolution fusion | flops 379857536 | bytes 23042888 | tf_op jit(solution)/shard_map/while/body/eval_jaxpr/hqk,qhd->khd/dot_general | solution.py:90
  878.3 2.8 fusion.185
  882.7 6.4 fusion.186
  889.0 21.8 %fusion.188 = bf16[8,64,584]{2,1,0:T(8,128)(2,1)S(1)} fusion(bf16[584,8,64]{0,2,1:T(8,128)(2,1)S(1)} %bitcast.145, f32[8,584,584]{1,2,0:T(8,128)} %fusion.186, f32[8,584,584]{1,2,0:T(8,128)} %copy-done, f32[8,584]{1,0:T(8,128)S(1)} %dynamic-slice_bitcast_fusion.8, pred[584]{0:T(1024)(128)(4,1)S(1)} %compare_reduce_fusion.5), kind=kOutput, calls=%fused_computation.38.clone.1 | convolution fusion | flops 379857536 | bytes 23042888 | tf_op jit(solution)/shard_map/while/body/eval_jaxpr/hqk,khd->qhd/dot_general | solution.py:87
  910.9 21.9 %fusion.187 = bf16[8,64,584]{2,1,0:T(8,128)(2,1)S(1)} fusion(bf16[584,8,64]{0,2,1:T(8,128)(2,1)S(1)} %bitcast.143, f32[8,584,584]{1,2,0:T(8,128)} %fusion.186, f32[8,584,584]{1,2,0:T(8,128)} %copy-done, f32[8,584]{1,0:T(8,128)S(1)} %dynamic-slice_bitcast_fusion.8, pred[584]{0:T(1024)(128)(4,1)S(1)} %compare_reduce_fusion.5), kind=kOutput, calls=%fused_computation.37.clone.1 | convolution fusion | flops 379857536 | bytes 23042888 | tf_op jit(solution)/shard_map/while/body/eval_jaxpr/hqk,qhd->khd/dot_general | solution.py:90
  934.4 13.4 copy.110
  947.8 6.7 all-to-all-start.3
  958.2 143.0 %all-to-all-done.3 = bf16[3,584,3,512]{3,2,0,1:T(4,128)(2,1)} async-done(((bf16[3,584,3,512]{3,2,0,1:T(4,128)(2,1)}), bf16[3,584,3,512]{3,2,0,1:T(4,128)(2,1)}, u32[]{:S(2)}, u32[]{:S(2)}) %all-to-all-start.3) | async-done | bytes 5382176 | tf_op jit(solution)/shard_map/all_to_all | solution.py:191
  1101.2 4.6 convert_reduce_fusion.1
  1105.8 9.6 copy.112
  1115.5 12.9 reshape.298
  1128.4 12.1 fusion.112
  1142.0 18.8 %fusion.91 = f32[4096,1024]{1,0:T(8,128)} fusion(bf16[876,1024]{1,0:T(8,128)(2,1)S(1)} %copy-done.6, f32[876,4096]{1,0:T(8,128)} %fusion.90, f32[4096]{0:T(1024)S(1)} %copy-done.45), kind=kOutput, calls=%fused_computation.152 | convolution fusion | flops 7384301568 | bytes 32940032 | tf_op jit(solution)/shard_map/dot_general | solution.py:31
  1161.6 17.9 %fusion.89 = f32[4096,1024]{1,0:T(8,128)} fusion(bf16[876,4096]{1,0:T(8,128)(2,1)} %get-tuple-element.185, f32[876,1024]{1,0:T(8,128)} %copy-done.7, f32[1024]{0:T(1024)S(1)} %copy-done.51, f32[1024]{0:T(1024)S(1)} %copy-done.35, f32[876]{0:T(1024)S(1)} %copy-done.41, f32[876]{0:T(1024)S(1)} %copy-done.26), kind=kOutput, calls=%fused_computation.150 | convolution fusion | flops 7352905728 | bytes 27556704 | tf_op jit(solution)/shard_map/dot_general | solution.py:31
  1183.3 17.0 add_add_fusion.3
  1200.3 3.8 reshape.299
  1204.1 12.4 multiply_reduce_fusion.2
  1216.7 72.3 %all-reduce = bf16[12288]{0:T(1024)(128)(2,1)S(1)} all-reduce(f32[12288]{0:T(1024)S(1)} %constant_dynamic-update-slice_fusion.1), channel_id=6, replica_groups=mesh['seq'=2,'fsdp'=8,'dp'=2] {'seq','fsdp'}, use_global_device_ids=true, to_apply=%region_33.34.clone | all-reduce | flops 12288 | bytes 73728
  1289.0 4.9 psum.46
  1297.4 163.8 %reduce-scatter.11.cloned.1.call-done = f32[256,1024]{1,0:T(8,128)} async-done(((f32[4096,1024]{1,0:T(8,128)}), f32[256,1024]{1,0:T(8,128)}) %reduce-scatter.11.cloned.1.call-update) | async-done | bytes 1048592 | tf_op jit(solution)/shard_map/reduce_scatter | solution.py:222
  1463.3 183.6 %reduce-scatter.9.cloned.1.call-done = f32[256,1024]{1,0:T(8,128)} async-done(((f32[4096,1024]{1,0:T(8,128)}), f32[256,1024]{1,0:T(8,128)}) %reduce-scatter.9.cloned.1.call-update) | async-done | bytes 1048592 | tf_op jit(solution)/shard_map/reduce_scatter | solution.py:221
  1649.7 4.3 fusion.92
  1656.6 48.6 %all-reduce.4.cloned.1.call-done = (bf16[64,3072]{1,0:T(8,128)(2,1)}, bf16[64,1024]{1,0:T(8,128)(2,1)}, bf16[256,1024]{1,0:T(8,128)(2,1)}, bf16[256,1024]{1,0:T(8,128)(2,1)}) async-done(((bf16[64,3072]{1,0:T(8,128)(2,1)}, bf16[64,1024]{1,0:T(8,128)(2,1)}, bf16[256,1024]{1,0:T(8,128)(2,1)}, bf16[256,1024]{1,0:T(8,128)(2,1)}), (bf16[64,3072]{1,0:T(8,128)(2,1)}, bf16[64,1024]{1,0:T(8,128)(2,1)}, ...) | async-done | bytes 1572880 | tf_op jit(solution)/shard_map/psum | solution.py:225
  1715.7 3.7 reshape.300
  1719.4 34.1 %psum.47 = f32[]{:T(128)} all-reduce(f32[]{:T(128)S(6)} %add.246), channel_id=1, replica_groups=mesh['seq'=2,'fsdp'=8,'dp'=2] {'seq','fsdp'}, use_global_device_ids=true, to_apply=%region_36.37 | all-reduce | flops 1 | bytes 8 | tf_op jit(solution)/shard_map/psum | solution.py:239
  1757.4 3.5 fusion.101
  1761.0 3.7 fusion.95
  (251 shorter events, 102.2 us)
Async XLA Ops:
  7.2 6.7 copy-start.3
  7.2 75.0 %all-gather.6.cloned.1.call-start = ((), (), s32[]{:S(2)}) async-start(), calls=%async_computation.8 | async-start | bytes 6684672 | tf_op jit(solution)/shard_map/all_gather | solution.py:133
  9.3 558.3 %all-gather.10.cloned.1.call-start = ((), (), s32[]{:S(2)}) async-start(), calls=%async_computation.10 | async-start | bytes 2228224 | tf_op jit(solution)/shard_map/all_gather | solution.py:134
  11.0 564.3 %all-gather.12.cloned.1.call-start = ((), (), s32[]{:S(2)}) async-start(), calls=%async_computation.11 | async-start | bytes 8912896 | tf_op jit(solution)/shard_map/all_gather | solution.py:138
  16.4 77.1 %copy-start.22 = (f32[3,292]{1,0:T(4,128)}, f32[3,292]{1,0:T(4,128)S(1)}, u32[]{:S(2)}) copy-start(f32[3,292]{1,0:T(4,128)S(1)} %broadcast_multiply_fusion) | copy-start | bytes 10516
  16.5 77.0 %copy-start.36 = (f32[876]{0:T(1024)}, f32[876]{0:T(1024)S(1)}, u32[]{:S(2)}) copy-start(f32[876]{0:T(1024)S(1)} %div.108) | copy-start | bytes 10516
  17.8 23.4 %copy-start.31 = (f32[876]{0:T(1024)}, f32[876]{0:T(1024)S(1)}, u32[]{:S(2)}) copy-start(f32[876]{0:T(1024)S(1)} %add.227) | copy-start | bytes 10516
  17.8 75.7 %copy-start.38 = (f32[876]{0:T(1024)}, f32[876]{0:T(1024)S(1)}, u32[]{:S(2)}) copy-start(f32[876]{0:T(1024)S(1)} %rsqrt.26) | copy-start | bytes 10516
  42.4 51.1 %copy-start.27 = (f32[1024]{0:T(1024)}, f32[1024]{0:T(1024)S(1)}, u32[]{:S(2)}) copy-start(f32[1024]{0:T(1024)S(1)} %get-tuple-element.207) | copy-start | bytes 12292
  42.4 51.1 %copy-start.47 = (f32[1024]{0:T(1024)}, f32[1024]{0:T(1024)S(1)}, u32[]{:S(2)}) copy-start(f32[1024]{0:T(1024)S(1)} %get-tuple-element.206) | copy-start | bytes 12292
  127.8 7.7 copy-start.10
  127.8 317.2 %all-to-all-start = ((bf16[3,292,3,1024]{1,2,0,3:T(4,128)(2,1)}), bf16[3,292,3,1024]{1,2,0,3:T(4,128)(2,1)}, u32[]{:S(2)}, u32[]{:S(2)}) async-start(bf16[3,292,3,1024]{1,2,0,3:T(4,128)(2,1)} %copy.98), calls=%async_computation | async-start | bytes 18874368 | tf_op jit(solution)/shard_map/all_to_all | solution.py:158
  135.3 455.3 %all-gather.8.cloned.1.call-start = ((), (), s32[]{:S(2)}) async-start(), calls=%async_computation.9 | async-start | bytes 8912896 | tf_op jit(solution)/shard_map/all_gather | solution.py:139
  459.7 14.5 copy-start.24
  510.2 50.8 %all-to-all-start.1 = ((bf16[3,584,512]{2,0,1:T(4,128)(2,1)}), bf16[3,584,512]{2,0,1:T(4,128)(2,1)}, u32[]{:S(2)}, u32[]{:S(2)}) async-start(bf16[3,584,512]{2,0,1:T(4,128)(2,1)} %copy.102), calls=%async_computation.1 | async-start | bytes 4784128 | tf_op jit(solution)/shard_map/all_to_all | solution.py:160
  516.4 74.2 %copy-start.44 = (f32[4096]{0:T(1024)}, f32[4096]{0:T(1024)S(1)}, u32[]{:S(2)}) copy-start(f32[4096]{0:T(1024)S(1)} %slice.83) | copy-start | bytes 49156
  518.0 109.5 %copy-start.5 = (bf16[876,1024]{1,0:T(8,128)(2,1)}, bf16[876,1024]{1,0:T(8,128)(2,1)S(1)}, u32[]{:S(2)}) copy-start(bf16[876,1024]{1,0:T(8,128)(2,1)S(1)} %reshape.295) | copy-start | bytes 5382148
  563.2 4.5 copy-start.52
  567.6 7.7 copy-start.34
  567.7 7.7 copy-start.50
  573.0 53.2 %copy-start.25 = (f32[876]{0:T(1024)}, f32[876]{0:T(1024)S(1)}, u32[]{:S(2)}) copy-start(f32[876]{0:T(1024)S(1)} %broadcast_multiply_fusion.1) | copy-start | bytes 10516
  575.3 50.9 %copy-start.40 = (f32[876]{0:T(1024)}, f32[876]{0:T(1024)S(1)}, u32[]{:S(2)}) copy-start(f32[876]{0:T(1024)S(1)} %fusion.87) | copy-start | bytes 10516
  590.5 22.0 %copy-start.8 = (f32[876,1024]{1,0:T(8,128)S(1)}, f32[876,1024]{1,0:T(8,128)}, u32[]{:S(2)}) copy-start(f32[876,1024]{1,0:T(8,128)} %copy-done.7) | copy-start | bytes 10764292
  627.4 1.8 copy-start.1
  627.4 4.3 copy-start.57
  627.4 3.1 copy-start.29
  640.5 100.0 %all-to-all-start.2 = ((bf16[3,292,1024]{1,0,2:T(4,128)(2,1)}), bf16[3,292,1024]{1,0,2:T(4,128)(2,1)S(1)}, u32[]{:S(2)}, u32[]{:S(2)}) async-start(bf16[3,292,1024]{1,0,2:T(4,128)(2,1)} %copy.105), calls=%async_computation.2 | async-start | bytes 6291456 | tf_op jit(solution)/shard_map/all_to_all | solution.py:189
  644.5 649.4 %reduce-scatter.7.cloned.1.call-start = ((), (), s32[]{:S(2)}) async-start(), calls=%async_computation.13 | async-start | bytes 4456448 | tf_op jit(solution)/shard_map/reduce_scatter | solution.py:217
  756.0 4.4 copy-start
  817.2 4.4 copy-start
  878.3 4.4 copy-start
  947.8 6.8 copy-start.4
  947.8 6.8 copy-start.23
  947.8 6.8 copy-start.28
  947.8 6.8 copy-start.33
  947.8 6.8 copy-start.48
  947.8 153.4 %all-to-all-start.3 = ((bf16[3,584,3,512]{3,2,0,1:T(4,128)(2,1)}), bf16[3,584,3,512]{3,2,0,1:T(4,128)(2,1)}, u32[]{:S(2)}, u32[]{:S(2)}) async-start(bf16[3,584,3,512]{3,2,0,1:T(4,128)(2,1)} %copy.110), calls=%async_computation.3 | async-start | bytes 14352384 | tf_op jit(solution)/shard_map/all_to_all | solution.py:191
  954.5 341.0 %reduce-scatter.5.cloned.1.call-start = ((), (), s32[]{:S(2)}) async-start(), calls=%async_computation.12 | async-start | bytes 13369344 | tf_op jit(solution)/shard_map/reduce_scatter | solution.py:216
  1140.5 320.7 %reduce-scatter.11.cloned.1.call-start = ((), (), s32[]{:S(2)}) async-start(), calls=%async_computation.15 | async-start | bytes 17825792 | tf_op jit(solution)/shard_map/reduce_scatter | solution.py:222
  1160.8 486.1 %reduce-scatter.9.cloned.1.call-start = ((), (), s32[]{:S(2)}) async-start(), calls=%async_computation.14 | async-start | bytes 17825792 | tf_op jit(solution)/shard_map/reduce_scatter | solution.py:221
  1179.4 3.8 copy-start.49
  1179.5 525.7 %all-reduce.4.cloned.1.call-start = ((), (), s32[]{:S(2)}) async-start(), calls=%async_computation.16 | async-start | bytes 3145728 | tf_op jit(solution)/shard_map/psum | solution.py:225
  1200.3 3.8 copy-start.37
  1200.3 3.8 copy-start.39
  1204.0 12.5 copy-start.42
  1204.1 12.5 copy-start.54
  1204.1 12.5 copy-start.53
  1204.1 12.6 copy-start.43
  1216.5 433.1 %copy-start.32 = (f32[876]{0:T(1024)S(1)}, f32[876]{0:T(1024)}, u32[]{:S(2)}) copy-start(f32[876]{0:T(1024)} %copy-done.31) | copy-start | bytes 10516
  1649.6 4.3 copy-start.2
  1649.6 4.3 copy-start.30
  1656.5 97.7 %copy-start.46 = (f32[768]{0:T(1024)S(1)}, f32[768]{0:T(1024)}, u32[]{:S(2)}) copy-start(f32[768]{0:T(1024)} %param.31) | copy-start | bytes 9220
  1656.5 97.7 %copy-start.55 = (f32[768]{0:T(1024)S(1)}, f32[768]{0:T(1024)}, u32[]{:S(2)}) copy-start(f32[768]{0:T(1024)} %param.41) | copy-start | bytes 9220
  1656.5 97.7 %copy-start.56 = (f32[768]{0:T(1024)S(1)}, f32[768]{0:T(1024)}, u32[]{:S(2)}) copy-start(f32[768]{0:T(1024)} %param.36) | copy-start | bytes 9220
  1656.5 100.9 %copy-start.12 = (f32[64,3072]{1,0:T(8,128)S(1)}, f32[64,3072]{1,0:T(8,128)}, u32[]{:S(2)}) copy-start(f32[64,3072]{1,0:T(8,128)} %param.27) | copy-start | bytes 2359300
  1705.2 49.8 %copy-start.20 = (bf16[64,1024]{1,0:T(8,128)(2,1)S(1)}, bf16[64,1024]{1,0:T(8,128)(2,1)}, u32[]{:S(2)}) copy-start(bf16[64,1024]{1,0:T(8,128)(2,1)} %get-tuple-element.159) | copy-start | bytes 393220
  1719.4 41.5 %copy-start.9 = (f32[256,1024]{1,0:T(8,128)S(1)}, f32[256,1024]{1,0:T(8,128)}, u32[]{:S(2)}) copy-start(f32[256,1024]{1,0:T(8,128)} %param.29) | copy-start | bytes 3145732
  1719.4 41.5 %copy-start.11 = (f32[256,1024]{1,0:T(8,128)S(1)}, f32[256,1024]{1,0:T(8,128)}, u32[]{:S(2)}) copy-start(f32[256,1024]{1,0:T(8,128)} %param.30) | copy-start | bytes 3145732
  1719.4 41.6 %copy-start.13 = (bf16[256,1024]{1,0:T(8,128)(2,1)S(1)}, bf16[256,1024]{1,0:T(8,128)(2,1)}, u32[]{:S(2)}) copy-start(bf16[256,1024]{1,0:T(8,128)(2,1)} %get-tuple-element.160) | copy-start | bytes 1572868
  1754.3 6.7 copy-start.14
  1754.3 6.7 copy-start.16
  1754.3 6.7 copy-start.17
  1754.3 6.7 copy-start.18
  1754.3 6.7 copy-start.19
  (10 other events, 10.3 us)
Sparse Core Ops, SparseCore 0:
  10.9 71.2 all-gather.5
  85.1 40.6 all-gather.9
  128.7 207.7 all-gather.11
  339.3 107.4 all-gather.7
  651.1 106.3 reduce-scatter.6
  1140.6 138.3 reduce-scatter.4
  1281.4 179.7 reduce-scatter.10
  1463.6 183.2 reduce-scatter.8
  1650.2 54.9 all-reduce.3
where the time goes:
time: 1780 us; the launch traced here: 1770 us
  waiting for transfers between devices  1020 us (57%)
  matrix products  339 us (19%)
  local copies, waits for them, and re-layouts  168 us (9%)
  blocking collectives  135 us (8%)
  other arithmetic  65.3 us (4%)
  starting transfers between devices  24.1 us (1%)
  between operations  21.6 us (1%)
    all_to_all x1, waiting for transfers between devices, on_device(): lax.all_to_all(packed, 'seq', split_axis=3, concat_axis=1, tiled=True)  308 us
    reduce_scatter x1, waiting for transfers between devices, on_device(): lax.psum_scatter(grad_up_w, ('seq', 'fsdp'), scatter_dimension=0, tiled=T...  184 us
    reduce_scatter x1, waiting for transfers between devices, on_device(): lax.psum_scatter(grad_down_w, ('seq', 'fsdp'), scatter_dimension=0, tiled...  164 us
    all_to_all x1, waiting for transfers between devices, on_device(): lax.all_to_all(grad_packed_heads, 'seq', split_axis=1, concat_axis=3, til...  143 us
    all_to_all x1, waiting for transfers between devices, on_device(): lax.all_to_all(grad_mixed, 'seq', split_axis=2, concat_axis=1, tiled=True)  89.5 us
    unnamed x1, blocking collectives  72.3 us
    dot_general x3, matrix products, attend_back(): jnp.einsum('hqk,qhd->khd', grad_scores, queries, preferred_element_type=j...  65.8 us
    dot_general x3, matrix products, attend_back(): jnp.einsum('hqk,khd->qhd', grad_scores, key_rows, preferred_element_type=...  65.4 us
  transfers between devices with their start and end apart: 13, of which 8 were waited for; matrix products, arithmetic and copies ran while one was open for 27% of the time, Pallas kernels for 0%

commit v1 on v0

--- a/solution.py
+++ b/solution.py
@@ -222,7 +222,7 @@
         lax.psum_scatter(grad_down_w, ("seq", "fsdp"), scatter_dimension=0, tiled=True),
     )
     share_in, share_out, share_up, share_down, share_vec = (
-        lax.psum(share_in.astype(jnp.bfloat16), "dp").astype(jnp.float32),
+        jnp.sum(lax.all_gather(share_in.astype(jnp.bfloat16), "dp"), axis=0).astype(jnp.float32),
         lax.psum(share_out.astype(jnp.bfloat16), "dp").astype(jnp.float32),
         lax.psum(share_up.astype(jnp.bfloat16), "dp").astype(jnp.float32),
         lax.psum(share_down.astype(jnp.bfloat16), "dp").astype(jnp.float32),

time: 1780 us -> 1540 us (0.87)
  waiting for transfers between devices: 1020 us -> 745 us
  blocking collectives: 135 us -> 164 us
    reduce_scatter x1, waiting for transfers between devices: 184 us -> 0.01 us  [on_device(): lax.psum_scatter(grad_up_w, ('seq', 'fsdp'), scatter_dimension=0, tiled=T...]
    reduce_scatter x1, waiting for transfers between devices: 164 us -> 0.01 us  [on_device(): lax.psum_scatter(grad_down_w, ('seq', 'fsdp'), scatter_dimension=0, tiled...]
    all_to_all x1, waiting for transfers between devices: 143 us -> 228 us  [on_device(): lax.all_to_all(grad_packed_heads, 'seq', split_axis=1, concat_axis=3, til...]
    psum x1, waiting for transfers between devices: 48.6 us -> 30.4 us  [on_device(): lax.psum(share_out.astype(jnp.bfloat16), 'dp').astype(jnp.float32)]
  transfers between devices with their start and end apart: 13 -> 13, of which waited for: 8 -> 7; matrix products, arithmetic and copies ran while one was open for 27% -> 33% of each run, Pallas kernels for 0% -> 0%
where the time goes in v1:
time: 1540 us; the launch traced here: 1530 us
  waiting for transfers between devices  745 us (48%)
  matrix products  338 us (22%)
  local copies, waits for them, and re-layouts  169 us (11%)
  blocking collectives  164 us (11%)
  other arithmetic  71.6 us (5%)
  starting transfers between devices  24.3 us (2%)
  between operations  21.4 us (1%)
    all_to_all x1, waiting for transfers between devices, on_device(): lax.all_to_all(packed, 'seq', split_axis=3, concat_axis=1, tiled=True)  309 us
    all_to_all x1, waiting for transfers between devices, on_device(): lax.all_to_all(grad_packed_heads, 'seq', split_axis=1, concat_axis=3, til...  228 us
    all_to_all x1, waiting for transfers between devices, on_device(): lax.all_to_all(grad_mixed, 'seq', split_axis=2, concat_axis=1, tiled=True)  89.7 us
    unnamed x1, blocking collectives  85.7 us
    dot_general x3, matrix products, attend_back(): jnp.einsum('hqk,qhd->khd', grad_scores, queries, preferred_element_type=j...  65.7 us
    dot_general x3, matrix products, attend_back(): jnp.einsum('hqk,khd->qhd', grad_scores, key_rows, preferred_element_type=...  65.3 us
    dot_general x4, matrix products, by_columns(): lax.dot_general(former, latter, (((1,), (1,)), ((), ())), preferred_eleme...  55.4 us
    dot_general x4, matrix products, by_rows(): lax.dot_general(former, latter, (((0,), (0,)), ((), ())), preferred_eleme...  51.5 us
  transfers between devices with their start and end apart: 13, of which 7 were waited for; matrix products, arithmetic and copies ran while one was open for 33% of the time, Pallas kernels for 0%

profile of v1, /device:TPU:0, one launch (start us, length us, event | category | flops | bytes accessed | tf_op | source)
XLA Modules:
  0.0 1534.1 jit_solution(8874292483996392261)
XLA Ops:
  17.8 23.3 %all-gather.1 = bf16[16,1,768]{2,1,0:T(2,128)(2,1)S(1)} all-gather(bf16[1,1,768]{2,1,0:T(2,128)(2,1)S(1)} %reshape.303), channel_id=1, replica_groups=mesh['seq'=2,'fsdp'=8,'dp'=2] {'seq','fsdp'}, dimensions={0}, use_global_device_ids=true | all-gather | bytes 26112 | tf_op jit(solution)/shard_map/all_gather | solution.py:135
  42.4 39.8 %all-gather.7.cloned.1.call-done = bf16[1024,3072]{1,0:T(8,128)(2,1)} async-done(((bf16[64,3072]{1,0:T(8,128)(2,1)}), bf16[1024,3072]{1,0:T(8,128)(2,1)}) %all-gather.7.cloned.1.call-update) | async-done | bytes 6291472 | tf_op jit(solution)/shard_map/all_gather | solution.py:133
  82.2 11.2 add_convert_fusion
  93.5 16.3 %reshape.294 = bf16[3,292,3,1024]{3,2,1,0:T(4,128)(2,1)} reshape(bf16[876,3072]{1,0:T(8,128)(2,1)} %add_convert_fusion) | data formatting | bytes 10764288 | tf_op jit(solution)/shard_map/reshape | solution.py:157
  109.8 17.9 %copy.98 = bf16[3,292,3,1024]{1,2,0,3:T(4,128)(2,1)} copy(bf16[3,292,3,1024]{3,2,1,0:T(4,128)(2,1)} %reshape.294) | data formatting | bytes 10764288 | tf_op jit(solution)/shard_map/reshape | solution.py:157
  127.7 7.4 all-to-all-start
  136.4 308.5 %all-to-all-done = bf16[3,292,3,1024]{1,2,0,3:T(4,128)(2,1)} async-done(((bf16[3,292,3,1024]{1,2,0,3:T(4,128)(2,1)}), bf16[3,292,3,1024]{1,2,0,3:T(4,128)(2,1)}, u32[]{:S(2)}, u32[]{:S(2)}) %all-to-all-start) | async-done | bytes 5382176 | tf_op jit(solution)/shard_map/all_to_all | solution.py:158
  444.9 14.8 copy.135
  459.8 14.5 reshape.308
  474.3 34.4 %while.22 = (s32[]{:T(128)}, bf16[3,584,512]{1,2,0:T(8,128)(2,1)S(1)}, f32[3,8,584]{2,1,0:T(8,128)S(1)}, bf16[3,584,3,512]{1,3,2,0:T(8,128)(2,1)}, s32[3,584]{1,0:T(4,128)}, /*index=5*/s32[]{:T(128)}) while((s32[]{:T(128)}, bf16[3,584,512]{1,2,0:T(8,128)(2,1)S(1)}, f32[3,8,584]{2,1,0:T(8,128)S(1)}, bf16[3,584,3,512]{1,3,2,0:T(8,128)(2,1)}, ...), condition=%wide.region_5.6_spmd, body=%wide.region_2.5_spmd.sunk | while | flops 731518976 | bytes 43779996 | solution.py:159
  482.3 3.3 fusion.172
  488.4 2.8 fusion.170
  493.8 3.3 fusion.172
  505.2 3.3 fusion.172
  508.7 3.7 copy.102
  512.4 4.9 all-to-all-start.1
  520.4 42.2 %all-to-all-done.1 = bf16[3,584,512]{2,0,1:T(4,128)(2,1)} async-done(((bf16[3,584,512]{2,0,1:T(4,128)(2,1)}), bf16[3,584,512]{2,0,1:T(4,128)(2,1)}, u32[]{:S(2)}, u32[]{:S(2)}) %all-to-all-start.1) | async-done | bytes 1794080 | tf_op jit(solution)/shard_map/all_to_all | solution.py:160
  569.1 5.3 fusion.109
  576.9 15.2 fusion.90
  592.1 22.1 %convert_reduce_fusion = (f32[4096]{0:T(1024)}, bf16[876,4096]{1,0:T(8,128)(2,1)}) fusion(f32[876,4096]{1,0:T(8,128)} %fusion.90, f32[4096]{0:T(1024)S(1)} %slice.83, bf16[876,1024]{1,0:T(8,128)(2,1)S(1)} %reshape.295, bf16[4096,1024]{1,0:T(8,128)(2,1)} %all-gather.9.cloned.1.call-done), kind=kOutput, calls=%fused_computation.60 | convolution fusion | flops 7430942720 | bytes 31744000 | tf_op jit(solution)/shard_map/dot_general | solution.py:37
  614.2 13.7 multiply_reduce_fusion.3
  633.4 4.4 fusion.113
  637.8 18.0 %fusion.91 = f32[4096,1024]{1,0:T(8,128)} fusion(bf16[876,1024]{1,0:T(8,128)(2,1)S(1)} %reshape.295, f32[876,4096]{1,0:T(8,128)} %fusion.90, f32[4096]{0:T(1024)S(1)} %slice.83), kind=kOutput, calls=%fused_computation.152 | convolution fusion | flops 7384301568 | bytes 32940032 | tf_op jit(solution)/shard_map/dot_general | solution.py:31
  655.9 16.8 %fusion.89 = f32[4096,1024]{1,0:T(8,128)} fusion(bf16[876,4096]{1,0:T(8,128)(2,1)} %get-tuple-element.184, f32[876,1024]{1,0:T(8,128)} %copy-done.6, f32[1024]{0:T(1024)S(1)} %copy-done.47, f32[1024]{0:T(1024)S(1)} %copy-done.34, f32[876]{0:T(1024)S(1)} %fusion.87, f32[876]{0:T(1024)S(1)} %broadcast_multiply_fusion.1), kind=kOutput, calls=%fused_computation.150 | convolution fusion | flops 7352905728 | bytes 27556704 | tf_op jit(solution)/shard_map/dot_general | solution.py:31
  674.2 4.9 convolution_convert_fusion
  680.7 3.9 copy.105
  684.6 4.0 all-to-all-start.2
  688.5 89.7 %all-to-all-done.2 = bf16[3,292,1024]{1,0,2:T(4,128)(2,1)S(1)} async-done(((bf16[3,292,1024]{1,0,2:T(4,128)(2,1)}), bf16[3,292,1024]{1,0,2:T(4,128)(2,1)S(1)}, u32[]{:S(2)}, u32[]{:S(2)}) %all-to-all-start.2) | async-done | bytes 1794080 | tf_op jit(solution)/shard_map/all_to_all | solution.py:189
  778.3 4.2 copy.136
  782.5 5.8 reshape.306
  788.3 187.8 %while.23 = (s32[]{:T(128)}, bf16[3,584,3,512]{1,3,2,0:T(8,128)(2,1)}, bf16[3,584,3,512]{1,3,2,0:T(8,128)(2,1)}, s32[3,584]{1,0:T(4,128)}, f32[3,8,584]{2,1,0:T(8,128)}, /*index=5*/bf16[3,584,512]{1,2,0:T(8,128)(2,1)}, s32[]{:T(128)}) while((s32[]{:T(128)}, bf16[3,584,3,512]{1,3,2,0:T(8,128)(2,1)}, bf16[3,584,3,512]{1,3,2,0:T(8,128)(2,1)}, ...), condition=%wide.region_12.13_spmd, body=%wide.region_10.12_spmd.sunk | while | flops 1824034688 | bytes 138262480 | solution.py:190
  795.0 2.8 fusion.185
  799.3 6.4 fusion.186
  805.7 21.8 %fusion.188 = bf16[8,64,584]{2,1,0:T(8,128)(2,1)S(1)} fusion(bf16[584,8,64]{0,2,1:T(8,128)(2,1)S(1)} %bitcast.146, f32[8,584,584]{1,2,0:T(8,128)} %fusion.186, f32[8,584,584]{1,2,0:T(8,128)} %copy-done, f32[8,584]{1,0:T(8,128)S(1)} %dynamic-slice_bitcast_fusion.8, pred[584]{0:T(1024)(128)(4,1)S(1)} %compare_reduce_fusion.5), kind=kOutput, calls=%fused_computation.38.clone.1 | convolution fusion | flops 379857536 | bytes 23042888 | tf_op jit(solution)/shard_map/while/body/eval_jaxpr/hqk,khd->qhd/dot_general | solution.py:87
  827.5 21.9 %fusion.187 = bf16[8,64,584]{2,1,0:T(8,128)(2,1)S(1)} fusion(bf16[584,8,64]{0,2,1:T(8,128)(2,1)S(1)} %bitcast.144, f32[8,584,584]{1,2,0:T(8,128)} %fusion.186, f32[8,584,584]{1,2,0:T(8,128)} %copy-done, f32[8,584]{1,0:T(8,128)S(1)} %dynamic-slice_bitcast_fusion.8, pred[584]{0:T(1024)(128)(4,1)S(1)} %compare_reduce_fusion.5), kind=kOutput, calls=%fused_computation.37.clone.1 | convolution fusion | flops 379857536 | bytes 23042888 | tf_op jit(solution)/shard_map/while/body/eval_jaxpr/hqk,qhd->khd/dot_general | solution.py:90
  857.5 2.8 fusion.185
  861.8 6.4 fusion.186
  868.2 21.8 %fusion.188 = bf16[8,64,584]{2,1,0:T(8,128)(2,1)S(1)} fusion(bf16[584,8,64]{0,2,1:T(8,128)(2,1)S(1)} %bitcast.146, f32[8,584,584]{1,2,0:T(8,128)} %fusion.186, f32[8,584,584]{1,2,0:T(8,128)} %copy-done, f32[8,584]{1,0:T(8,128)S(1)} %dynamic-slice_bitcast_fusion.8, pred[584]{0:T(1024)(128)(4,1)S(1)} %compare_reduce_fusion.5), kind=kOutput, calls=%fused_computation.38.clone.1 | convolution fusion | flops 379857536 | bytes 23042888 | tf_op jit(solution)/shard_map/while/body/eval_jaxpr/hqk,khd->qhd/dot_general | solution.py:87
  890.0 21.9 %fusion.187 = bf16[8,64,584]{2,1,0:T(8,128)(2,1)S(1)} fusion(bf16[584,8,64]{0,2,1:T(8,128)(2,1)S(1)} %bitcast.144, f32[8,584,584]{1,2,0:T(8,128)} %fusion.186, f32[8,584,584]{1,2,0:T(8,128)} %copy-done, f32[8,584]{1,0:T(8,128)S(1)} %dynamic-slice_bitcast_fusion.8, pred[584]{0:T(1024)(128)(4,1)S(1)} %compare_reduce_fusion.5), kind=kOutput, calls=%fused_computation.37.clone.1 | convolution fusion | flops 379857536 | bytes 23042888 | tf_op jit(solution)/shard_map/while/body/eval_jaxpr/hqk,qhd->khd/dot_general | solution.py:90
  920.0 2.8 fusion.185
  924.3 6.4 fusion.186
  930.7 21.8 %fusion.188 = bf16[8,64,584]{2,1,0:T(8,128)(2,1)S(1)} fusion(bf16[584,8,64]{0,2,1:T(8,128)(2,1)S(1)} %bitcast.146, f32[8,584,584]{1,2,0:T(8,128)} %fusion.186, f32[8,584,584]{1,2,0:T(8,128)} %copy-done, f32[8,584]{1,0:T(8,128)S(1)} %dynamic-slice_bitcast_fusion.8, pred[584]{0:T(1024)(128)(4,1)S(1)} %compare_reduce_fusion.5), kind=kOutput, calls=%fused_computation.38.clone.1 | convolution fusion | flops 379857536 | bytes 23042888 | tf_op jit(solution)/shard_map/while/body/eval_jaxpr/hqk,khd->qhd/dot_general | solution.py:87
  952.5 21.9 %fusion.187 = bf16[8,64,584]{2,1,0:T(8,128)(2,1)S(1)} fusion(bf16[584,8,64]{0,2,1:T(8,128)(2,1)S(1)} %bitcast.144, f32[8,584,584]{1,2,0:T(8,128)} %fusion.186, f32[8,584,584]{1,2,0:T(8,128)} %copy-done, f32[8,584]{1,0:T(8,128)S(1)} %dynamic-slice_bitcast_fusion.8, pred[584]{0:T(1024)(128)(4,1)S(1)} %compare_reduce_fusion.5), kind=kOutput, calls=%fused_computation.37.clone.1 | convolution fusion | flops 379857536 | bytes 23042888 | tf_op jit(solution)/shard_map/while/body/eval_jaxpr/hqk,qhd->khd/dot_general | solution.py:90
  976.1 13.4 copy.110
  989.5 6.7 all-to-all-start.3
  999.9 228.1 %all-to-all-done.3 = bf16[3,584,3,512]{3,2,0,1:T(4,128)(2,1)} async-done(((bf16[3,584,3,512]{3,2,0,1:T(4,128)(2,1)}), bf16[3,584,3,512]{3,2,0,1:T(4,128)(2,1)}, u32[]{:S(2)}, u32[]{:S(2)}) %all-to-all-start.3) | async-done | bytes 5382176 | tf_op jit(solution)/shard_map/all_to_all | solution.py:191
  1228.1 4.7 convert_reduce_fusion.1
  1232.8 9.7 copy.112
  1242.5 12.9 reshape.298
  1255.4 12.3 fusion.112
  1270.2 17.4 %add_add_fusion.3 = f32[876,1024]{1,0:T(8,128)} fusion(f32[876,1024]{1,0:T(8,128)} %copy-done.6, f32[1024]{0:T(1024)S(1)} %copy-done.46, bf16[4096,1024]{1,0:T(8,128)(2,1)} %all-gather.9.cloned.1.call-done, f32[876,4096]{1,0:T(8,128)} %fusion.90, f32[4096]{0:T(1024)S(1)} %copy-done.42), kind=kOutput, calls=%fused_computation.73 | convolution fusion | flops 7386095616 | bytes 29937664 | tf_op jit(solution)/shard_map/dot_general | solution.py:27
  1287.6 4.0 reshape.299
  1291.7 13.2 multiply_reduce_fusion.2
  1305.0 85.7 %all-reduce = bf16[12288]{0:T(1024)(128)(2,1)S(1)} all-reduce(f32[12288]{0:T(1024)S(1)} %constant_dynamic-update-slice_fusion.1), channel_id=7, replica_groups=mesh['seq'=2,'fsdp'=8,'dp'=2] {'seq','fsdp'}, use_global_device_ids=true, to_apply=%region_33.34.clone | all-reduce | flops 12288 | bytes 73728
  1390.8 5.3 psum.38
  1396.1 6.2 fusion.92
  1408.7 5.7 add_add_fusion.2
  1414.4 6.3 reduce-scatter.5.cloned.1.call-done
  1422.0 15.3 all-gather
  1438.4 30.4 %all-reduce.4.cloned.1.call-done = (bf16[64,1024]{1,0:T(8,128)(2,1)}, bf16[256,1024]{1,0:T(8,128)(2,1)}, bf16[256,1024]{1,0:T(8,128)(2,1)}) async-done(((bf16[64,1024]{1,0:T(8,128)(2,1)}, bf16[256,1024]{1,0:T(8,128)(2,1)}, bf16[256,1024]{1,0:T(8,128)(2,1)}), (bf16[64,1024]{1,0:T(8,128)(2,1)}, bf16[256,1024]{1,0:T(8,128)(2,1)}, bf16[256,1024]{1,0:T(8,128)(2,1)})) %all-reduce.4.cloned.1.call-update) | async-done | bytes 1179664 | tf_op jit(solution)/shard_map/psum | solution.py:226
  1477.4 3.7 reshape.300
  1481.2 33.9 %psum.39 = f32[]{:T(128)} all-reduce(f32[]{:T(128)S(6)} %add.244), channel_id=1, replica_groups=mesh['seq'=2,'fsdp'=8,'dp'=2] {'seq','fsdp'}, use_global_device_ids=true, to_apply=%region_36.37 | all-reduce | flops 1 | bytes 8 | tf_op jit(solution)/shard_map/psum | solution.py:239
  1519.1 3.4 fusion.101
  1522.5 3.7 fusion.95
  (243 shorter events, 105.8 us)
Async XLA Ops:
  7.2 6.7 copy-start.2
  7.2 75.0 %all-gather.7.cloned.1.call-start = ((), (), s32[]{:S(2)}) async-start(), calls=%async_computation.8 | async-start | bytes 6684672 | tf_op jit(solution)/shard_map/all_gather | solution.py:133
  9.3 559.8 %all-gather.11.cloned.1.call-start = ((), (), s32[]{:S(2)}) async-start(), calls=%async_computation.10 | async-start | bytes 2228224 | tf_op jit(solution)/shard_map/all_gather | solution.py:134
  11.0 565.8 %all-gather.13.cloned.1.call-start = ((), (), s32[]{:S(2)}) async-start(), calls=%async_computation.11 | async-start | bytes 8912896 | tf_op jit(solution)/shard_map/all_gather | solution.py:138
  16.4 77.1 %copy-start.25 = (f32[3,292]{1,0:T(4,128)}, f32[3,292]{1,0:T(4,128)S(1)}, u32[]{:S(2)}) copy-start(f32[3,292]{1,0:T(4,128)S(1)} %broadcast_multiply_fusion) | copy-start | bytes 10516
  16.5 77.0 %copy-start.35 = (f32[876]{0:T(1024)}, f32[876]{0:T(1024)S(1)}, u32[]{:S(2)}) copy-start(f32[876]{0:T(1024)S(1)} %div.108) | copy-start | bytes 10516
  17.8 23.4 %copy-start.31 = (f32[876]{0:T(1024)}, f32[876]{0:T(1024)S(1)}, u32[]{:S(2)}) copy-start(f32[876]{0:T(1024)S(1)} %add.225) | copy-start | bytes 10516
  17.8 75.7 %copy-start.37 = (f32[876]{0:T(1024)}, f32[876]{0:T(1024)S(1)}, u32[]{:S(2)}) copy-start(f32[876]{0:T(1024)S(1)} %rsqrt.26) | copy-start | bytes 10516
  42.4 51.1 %copy-start.27 = (f32[1024]{0:T(1024)}, f32[1024]{0:T(1024)S(1)}, u32[]{:S(2)}) copy-start(f32[1024]{0:T(1024)S(1)} %get-tuple-element.206) | copy-start | bytes 12292
  42.4 51.1 %copy-start.44 = (f32[1024]{0:T(1024)}, f32[1024]{0:T(1024)S(1)}, u32[]{:S(2)}) copy-start(f32[1024]{0:T(1024)S(1)} %get-tuple-element.205) | copy-start | bytes 12292
  127.7 7.8 copy-start.10
  127.7 317.2 %all-to-all-start = ((bf16[3,292,3,1024]{1,2,0,3:T(4,128)(2,1)}), bf16[3,292,3,1024]{1,2,0,3:T(4,128)(2,1)}, u32[]{:S(2)}, u32[]{:S(2)}) async-start(bf16[3,292,3,1024]{1,2,0,3:T(4,128)(2,1)} %copy.98), calls=%async_computation | async-start | bytes 18874368 | tf_op jit(solution)/shard_map/all_to_all | solution.py:158
  135.2 456.9 %all-gather.9.cloned.1.call-start = ((), (), s32[]{:S(2)}) async-start(), calls=%async_computation.9 | async-start | bytes 8912896 | tf_op jit(solution)/shard_map/all_gather | solution.py:139
  508.7 11.6 copy-start.24
  512.4 50.1 %all-to-all-start.1 = ((bf16[3,584,512]{2,0,1:T(4,128)(2,1)}), bf16[3,584,512]{2,0,1:T(4,128)(2,1)}, u32[]{:S(2)}, u32[]{:S(2)}) async-start(bf16[3,584,512]{2,0,1:T(4,128)(2,1)} %copy.102), calls=%async_computation.1 | async-start | bytes 4784128 | tf_op jit(solution)/shard_map/all_to_all | solution.py:160
  517.4 884.9 %reduce-scatter.7.cloned.1.call-start = ((), (), s32[]{:S(2)}) async-start(), calls=%async_computation.13 | async-start | bytes 4456448 | tf_op jit(solution)/shard_map/reduce_scatter | solution.py:217
  518.7 119.1 %copy-start.41 = (f32[4096]{0:T(1024)}, f32[4096]{0:T(1024)S(1)}, u32[]{:S(2)}) copy-start(f32[4096]{0:T(1024)S(1)} %slice.83) | copy-start | bytes 49156
  520.3 117.5 %copy-start.4 = (bf16[876,1024]{1,0:T(8,128)(2,1)}, bf16[876,1024]{1,0:T(8,128)(2,1)S(1)}, u32[]{:S(2)}) copy-start(bf16[876,1024]{1,0:T(8,128)(2,1)S(1)} %reshape.295) | copy-start | bytes 5382148
  564.6 4.5 copy-start.48
  569.1 7.7 copy-start.34
  569.1 7.7 copy-start.47
  592.1 22.1 %copy-start.7 = (f32[876,1024]{1,0:T(8,128)S(1)}, f32[876,1024]{1,0:T(8,128)}, u32[]{:S(2)}) copy-start(f32[876,1024]{1,0:T(8,128)} %copy-done.6) | copy-start | bytes 10764292
  629.0 1.8 copy-start.1
  629.1 4.3 copy-start.17
  629.1 3.1 copy-start.29
  637.7 766.2 %reduce-scatter.11.cloned.1.call-start = ((), (), s32[]{:S(2)}) async-start(), calls=%async_computation.15 | async-start | bytes 17825792 | tf_op jit(solution)/shard_map/reduce_scatter | solution.py:222
  655.9 750.1 %reduce-scatter.9.cloned.1.call-start = ((), (), s32[]{:S(2)}) async-start(), calls=%async_computation.14 | async-start | bytes 17825792 | tf_op jit(solution)/shard_map/reduce_scatter | solution.py:221
  684.6 93.7 %all-to-all-start.2 = ((bf16[3,292,1024]{1,0,2:T(4,128)(2,1)}), bf16[3,292,1024]{1,0,2:T(4,128)(2,1)S(1)}, u32[]{:S(2)}, u32[]{:S(2)}) async-start(bf16[3,292,1024]{1,0,2:T(4,128)(2,1)} %copy.105), calls=%async_computation.2 | async-start | bytes 6291456 | tf_op jit(solution)/shard_map/all_to_all | solution.py:189
  795.0 4.3 copy-start
  857.5 4.3 copy-start
  920.0 4.3 copy-start
  989.5 6.8 copy-start.3
  989.5 6.8 copy-start.26
  989.5 6.8 copy-start.28
  989.5 6.8 copy-start.33
  989.5 6.8 copy-start.45
  989.5 238.6 %all-to-all-start.3 = ((bf16[3,584,3,512]{3,2,0,1:T(4,128)(2,1)}), bf16[3,584,3,512]{3,2,0,1:T(4,128)(2,1)}, u32[]{:S(2)}, u32[]{:S(2)}) async-start(bf16[3,584,3,512]{3,2,0,1:T(4,128)(2,1)} %copy.110), calls=%async_computation.3 | async-start | bytes 14352384 | tf_op jit(solution)/shard_map/all_to_all | solution.py:191
  996.2 424.5 %reduce-scatter.5.cloned.1.call-start = ((), (), s32[]{:S(2)}) async-start(), calls=%async_computation.12 | async-start | bytes 13369344 | tf_op jit(solution)/shard_map/reduce_scatter | solution.py:216
  1267.7 2.1 copy-start.8
  1267.7 2.5 copy-start.42
  1267.7 2.5 copy-start.46
  1267.7 201.1 %all-reduce.4.cloned.1.call-start = ((), (), s32[]{:S(2)}) async-start(), calls=%async_computation.16 | async-start | bytes 2359296 | tf_op jit(solution)/shard_map/psum | solution.py:226
  1287.6 4.0 copy-start.36
  1287.6 4.0 copy-start.38
  1291.6 13.3 copy-start.39
  1291.6 13.3 copy-start.50
  1291.6 13.3 copy-start.49
  1291.7 13.3 copy-start.40
  1291.7 104.4 %copy-start.32 = (f32[876]{0:T(1024)S(1)}, f32[876]{0:T(1024)}, u32[]{:S(2)}) copy-start(f32[876]{0:T(1024)} %copy-done.31) | copy-start | bytes 10516
  1396.1 12.6 copy-start.5
  1396.1 12.6 copy-start.30
  1421.9 93.9 %copy-start.43 = (f32[768]{0:T(1024)S(1)}, f32[768]{0:T(1024)}, u32[]{:S(2)}) copy-start(f32[768]{0:T(1024)} %param.31) | copy-start | bytes 9220
  1422.0 93.9 %copy-start.51 = (f32[768]{0:T(1024)S(1)}, f32[768]{0:T(1024)}, u32[]{:S(2)}) copy-start(f32[768]{0:T(1024)} %param.41) | copy-start | bytes 9220
  1422.0 93.9 %copy-start.52 = (f32[768]{0:T(1024)S(1)}, f32[768]{0:T(1024)}, u32[]{:S(2)}) copy-start(f32[768]{0:T(1024)} %param.36) | copy-start | bytes 9220
  1422.0 94.6 %copy-start.18 = (f32[64,1024]{1,0:T(8,128)S(1)}, f32[64,1024]{1,0:T(8,128)}, u32[]{:S(2)}) copy-start(f32[64,1024]{1,0:T(8,128)} %param.28) | copy-start | bytes 786436
  1437.6 81.5 %copy-start.12 = (f32[64,3072]{1,0:T(8,128)S(1)}, f32[64,3072]{1,0:T(8,128)}, u32[]{:S(2)}) copy-start(f32[64,3072]{1,0:T(8,128)} %param.27) | copy-start | bytes 2359300
  1481.2 41.3 %copy-start.9 = (f32[256,1024]{1,0:T(8,128)S(1)}, f32[256,1024]{1,0:T(8,128)}, u32[]{:S(2)}) copy-start(f32[256,1024]{1,0:T(8,128)} %param.29) | copy-start | bytes 3145732
  1481.2 41.3 %copy-start.11 = (f32[256,1024]{1,0:T(8,128)S(1)}, f32[256,1024]{1,0:T(8,128)}, u32[]{:S(2)}) copy-start(f32[256,1024]{1,0:T(8,128)} %param.30) | copy-start | bytes 3145732
  1515.9 6.6 copy-start.13
  1515.9 6.6 copy-start.14
  1515.9 6.6 copy-start.19
  1515.9 6.6 copy-start.20
  1515.9 6.6 copy-start.21
  1516.0 6.6 copy-start.22
  (5 other events, 6.1 us)
Sparse Core Ops, SparseCore 0:
  10.9 71.2 all-gather.6
  85.1 40.6 all-gather.10
  128.7 207.7 all-gather.12
  339.2 107.4 all-gather.8
  637.9 110.9 reduce-scatter.6
  751.0 188.6 reduce-scatter.10
  942.0 336.6 reduce-scatter.8
  1283.4 137.3 reduce-scatter.4
  1424.0 44.7 all-reduce.3
